TPU v7x, 32 devices: a whole 2x2x4 slice. The times are simulated.
32 devices in a mesh: lat: 4 (over x, core), lon: 8 (over z, y).
Axes of the slice: x: 2, y: 2, z: 4, core: 2. Of those that a mesh axis runs over, the one named last changes fastest.
Arguments:
- mesh_nodes: bfloat16 [8192, 512], P(('lat', 'lon')), may hold values from -6 to 6
- mesh_edges: bfloat16 [65536, 512], P(('lat', 'lon')), may hold values from -6 to 6
- grid_state: bfloat16 [128, 256, 512], P('lat', 'lon'), may hold values from -6 to 6
- decoder_edges: bfloat16 [3, 128, 256, 512], P(None, 'lat', 'lon'), may hold values from -6 to 6
- edge_send: int32 [65536], P(('lat', 'lon')), may hold values from 0 to 511
- edge_recv: int32 [65536], P(('lat', 'lon')), may hold values from -1 to 255, as said below
- halo_lists: int32 [32, 32, 8], P(('lat', 'lon')), may hold values from 0 to 255
- decoder_lists: int32 [32, 32, 4], P(('lat', 'lon')), may hold values from 0 to 255
- decoder_sources: int32 [3, 128, 256], P(None, 'lat', 'lon'), may hold values from 0 to 127
- edge_first: bfloat16 [2, 1536, 512], replicated, may hold values from -0.15625 to 0.15625
- edge_second: bfloat16 [2, 512, 512], replicated, may hold values from -0.25 to 0.25
- node_first: bfloat16 [2, 1024, 512], replicated, may hold values from -0.1875 to 0.1875
- node_second: bfloat16 [2, 512, 512], replicated, may hold values from -0.25 to 0.25
- decoder_first: bfloat16 [1536, 512], replicated, may hold values from -0.15625 to 0.15625
- decoder_second: bfloat16 [512, 512], replicated, may hold values from -0.25 to 0.25
- grid_first: bfloat16 [1024, 512], replicated, may hold values from -0.1875 to 0.1875
- grid_second: bfloat16 [512, 512], replicated, may hold values from -0.25 to 0.25
Outputs:
- mesh_final: bfloat16 [8192, 512], P(('lat', 'lon'))
- grid_final: bfloat16 [128, 256, 512], P('lat', 'lon')
Inputs may be any that keep to these rules, and one draw needn't show every extreme that they name: `edge_recv`: on each partition the live edges come first; their number is a multiple of 128, at least 128 and at most 2048, and some partition has 2048; live receivers are local node rows, padding slots hold -1.
All inputs are finite; a program needn't handle non-finite values.
Results may differ from a plain program's by a relative error of at most 0.012.
Values may be sent and summed in bfloat16 or wider, within the bound.
A program may use at most 128 MiB of HBM per device.

v0:
```python
import jax
import jax.numpy as jnp
from jax import lax
from jax.sharding import PartitionSpec as P

epsilon = 1e-05


def normalize(values):
    average = jnp.mean(values, axis=-1, keepdims=True)
    centered = values - average
    spread = jnp.mean(centered * centered, axis=-1, keepdims=True)
    return centered * lax.rsqrt(spread + epsilon)


def perceptron(inputs, layer_one, layer_two):
    hidden = jax.nn.silu(jnp.dot(inputs, layer_one, preferred_element_type=jnp.float32)).astype(
        jnp.bfloat16
    )
    return normalize(jnp.dot(hidden, layer_two, preferred_element_type=jnp.float32))


def pick_rows(indices, lookup):
    table_rows = lookup.shape[0]
    picker = (indices[:, None] == jnp.arange(table_rows, dtype=jnp.int32)[None, :]).astype(
        jnp.bfloat16
    )
    return (
        picker,
        jnp.dot(picker, lookup, preferred_element_type=jnp.float32).astype(jnp.bfloat16),
    )


def mesh_route(outgoing):
    return lax.all_to_all(outgoing, ("lat", "lon"), split_axis=0, concat_axis=0, tiled=True)


def decoder_route(outgoing):
    return lax.all_to_all(outgoing, ("lat", "lon"), split_axis=0, concat_axis=0, tiled=True)


def mesh_layer(
    nodes_now, edges_now, edge_send, edge_recv, send_lists, w_edge1, w_edge2, w_node1, w_node2
):
    node_count, feature_width = nodes_now.shape
    flat_rows = send_lists.reshape(-1)
    ignored, outgoing = pick_rows(flat_rows, nodes_now)
    outgoing = outgoing.reshape(send_lists.shape[1], send_lists.shape[2], feature_width)
    incoming = mesh_route(outgoing).reshape(-1, feature_width)
    lookup = jnp.concatenate([nodes_now, incoming], axis=0)
    edge_count = edges_now.shape[0]
    block_rows = 512
    live_edges = jnp.sum((edge_recv >= 0).astype(jnp.int32))
    block_count = (live_edges + block_rows - 1) // block_rows

    def mesh_advance(number, carry):
        summed, updated = carry
        first_row = number * block_rows
        edge_block = lax.dynamic_slice_in_dim(edges_now, first_row, block_rows, 0)
        senders = lax.dynamic_slice_in_dim(edge_send, first_row, block_rows, 0)
        targets = lax.dynamic_slice_in_dim(edge_recv, first_row, block_rows, 0)
        ignored_send, from_send = pick_rows(senders, lookup)
        pick_recv, from_recv = pick_rows(targets, nodes_now)
        result = perceptron(
            jnp.concatenate([edge_block, from_send, from_recv], axis=1), w_edge1, w_edge2
        )
        message = result.astype(jnp.bfloat16)
        summed = summed + lax.dot_general(
            pick_recv, message, (((0,), (0,)), ((), ())), preferred_element_type=jnp.float32
        )
        fresh = (edge_block.astype(jnp.float32) + result).astype(jnp.bfloat16)
        updated = lax.dynamic_update_slice_in_dim(updated, fresh, first_row, 0)
        return (summed, updated)

    start_sum = jnp.zeros((node_count, feature_width), jnp.float32)
    summed, fresh_edges = lax.fori_loop(0, block_count, mesh_advance, (start_sum, edges_now))
    gathered = summed.astype(jnp.bfloat16)
    result = perceptron(jnp.concatenate([nodes_now, gathered], axis=1), w_node1, w_node2)
    fresh_nodes = (nodes_now.astype(jnp.float32) + result).astype(jnp.bfloat16)
    return (fresh_nodes, fresh_edges)


def decode(
    nodes_now,
    grid_state,
    decoder_edges,
    decoder_sources,
    decoder_lists,
    decoder_first,
    decoder_second,
    grid_first,
    grid_second,
):
    feature_width = nodes_now.shape[1]
    ignored, outgoing = pick_rows(decoder_lists.reshape(-1), nodes_now)
    outgoing = outgoing.reshape(decoder_lists.shape[1], decoder_lists.shape[2], feature_width)
    lookup = decoder_route(outgoing).reshape(-1, feature_width)
    tile_lat, tile_lon = (grid_state.shape[0], grid_state.shape[1])
    cells = tile_lat * tile_lon
    flat_grid = grid_state.reshape(cells, feature_width)
    flat_edges = decoder_edges.reshape(3, cells, feature_width)
    flat_sources = decoder_sources.reshape(3, cells)
    block_rows = 512

    def decode_advance(number, updated):
        first_row = number * block_rows
        grid_block = lax.dynamic_slice_in_dim(flat_grid, first_row, block_rows, 0)
        summed = jnp.zeros((block_rows, feature_width), jnp.float32)
        for branch in range(3):
            sources = lax.dynamic_slice_in_dim(flat_sources[branch], first_row, block_rows, 0)
            ignored_pick, mesh_rows = pick_rows(sources, lookup)
            edge_block = lax.dynamic_slice_in_dim(flat_edges[branch], first_row, block_rows, 0)
            result = perceptron(
                jnp.concatenate([edge_block, mesh_rows, grid_block], axis=1),
                decoder_first,
                decoder_second,
            )
            summed = summed + lax.optimization_barrier(result.astype(jnp.bfloat16)).astype(
                jnp.float32
            )
        gathered = summed.astype(jnp.bfloat16)
        result = perceptron(
            jnp.concatenate([grid_block, gathered], axis=1), grid_first, grid_second
        )
        fresh = (grid_block.astype(jnp.float32) + result).astype(jnp.bfloat16)
        return lax.dynamic_update_slice_in_dim(updated, fresh, first_row, 0)

    decoded = lax.fori_loop(0, cells // block_rows, decode_advance, flat_grid)
    return decoded.reshape(tile_lat, tile_lon, feature_width)


def shards(
    mesh_nodes,
    mesh_edges,
    grid_state,
    decoder_edges,
    edge_send,
    edge_recv,
    halo_lists,
    decoder_lists,
    decoder_sources,
    edge_first,
    edge_second,
    node_first,
    node_second,
    decoder_first,
    decoder_second,
    grid_first,
    grid_second,
):
    nodes_now, edges_now = (mesh_nodes, mesh_edges)
    for layer in range(edge_first.shape[0]):
        nodes_now, edges_now = mesh_layer(
            nodes_now,
            edges_now,
            edge_send,
            edge_recv,
            halo_lists,
            edge_first[layer],
            edge_second[layer],
            node_first[layer],
            node_second[layer],
        )
    grid_final = decode(
        nodes_now,
        grid_state,
        decoder_edges,
        decoder_sources,
        decoder_lists,
        decoder_first,
        decoder_second,
        grid_first,
        grid_second,
    )
    return (nodes_now, grid_final)


def solution(mesh):
    placed = (
        P(("lat", "lon"), None),
        P(("lat", "lon"), None),
        P("lat", "lon", None),
        P(None, "lat", "lon", None),
        P(("lat", "lon")),
        P(("lat", "lon")),
        P(("lat", "lon"), None, None),
        P(("lat", "lon"), None, None),
        P(None, "lat", "lon"),
        P(),
        P(),
        P(),
        P(),
        P(),
        P(),
        P(),
        P(),
    )
    return jax.shard_map(
        shards,
        mesh=mesh,
        in_specs=placed,
        out_specs=(P(("lat", "lon"), None), P("lat", "lon", None)),
        check_vma=False,
    )
```

profile of v0, /device:TPU:0, one launch (start us, length us, event | category | flops | bytes accessed | tf_op | source)
XLA Modules:
  0.0 212.8 jit_solution(7518035032993915175)
XLA Ops:
  1.5 1.9 fusion.88
  3.4 7.3 %all-to-all-start = ((bf16[32,8,512]{2,1,0:T(8,128)(2,1)}), bf16[32,8,512]{2,1,0:T(8,128)(2,1)S(1)}, u32[]{:S(2)}, u32[]{:S(2)}) async-start(bf16[32,8,512]{2,1,0:T(8,128)(2,1)} %fusion.88), calls=%async_computation | async-start | bytes 524288 | tf_op jit(solution)/shard_map/all_to_all | solution.py:35
  10.7 1.3 convert_reduce_fusion
  12.8 4.1 %copy.27 = bf16[2048,512]{0,1:T(8,128)(2,1)} copy(bf16[2048,512]{1,0:T(8,128)(2,1)} %param.24) | data formatting | bytes 4194304 | tf_op jit(solution)/shard_map/while | solution.py:76
  17.9 3.8 %slice_bitcast_fusion = (bf16[1536,512]{1,0:T(8,128)(2,1)}, bf16[1536,512]{1,0:T(8,128)(2,1)}) fusion(bf16[2,1536,512]{2,1,0:T(8,128)(2,1)} %param.32), kind=kLoop, calls=%fused_computation.129 | loop fusion | bytes 6291456 | tf_op jit(solution)/shard_map/squeeze | solution.py:159
  21.8 8.4 %while.37 = (s32[]{:T(128)}, f32[256,512]{1,0:T(8,128)S(1)}, bf16[2048,512]{0,1:T(8,128)(2,1)}, s32[]{:T(128)}, s32[2048]{0:T(1024)S(1)}, /*index=5*/bf16[2048,5...) while((s32[]{:T(128)}, f32[256,512]{1,0:T(8,128)S(1)}, ...), condition=%wide.region_4.5_spmd, body=%wide.region_1.4_spmd.sunk | while | flops 1621099008 | bytes 13930707 | solution.py:76
  22.5 1.5 convolution_convert_fusion.18
  23.9 1.1 constant_dynamic-slice_fusion.11
  25.2 3.2 %fusion.220 = (f32[512]{0:T(512)S(1)}, f32[512,512]{0,1:T(8,128)S(1)}) fusion(bf16[512,512]{1,0:T(8,128)(2,1)} %get-tuple-element.734, bf16[1536,512]{1,0:T(8,128)(2,1)} %get-tuple-element.733, bf16[512,512]{0,1:T(8,128)(2,1)S(1)} %convolution_convert_fusion.17, bf16[512,512]{0,1:T(8,128)(2,1)} %convolution_convert_fusion.18, ...), kind=kOutput, calls=%fused_computation.180.clone.1 | convolution fusion | flops 1080032768 | bytes 4720640 | tf_op jit(solution)/shard_map/while/body/dot_general | solution.py:20
  29.2 1.0 fusion.221
  30.2 2.2 %fusion.149 = (f32[256]{0:T(256)S(1)}, f32[256,512]{1,0:T(8,128)S(1)}) fusion(bf16[2,512,512]{2,1,0:T(8,128)(2,1)} %param.35, bf16[2,1024,512]{2,1,0:T(8,128)(2,1)} %param.34, bf16[256,512]{1,0:T(8,128)(2,1)S(1)} %convert_element_type.206, bf16[256,512]{1,0:T(8,128)(2,1)S(1)} %get-tuple-element.824), kind=kOutput, calls=%fused_computation.188 | convolution fusion | flops 404487936 | bytes 2622464 | tf_op jit(solution)/shard_map/dot_general | solution.py:20
  33.8 30.9 %all-to-all-start.1 = ((bf16[32,8,512]{2,1,0:T(8,128)(2,1)}), bf16[32,8,512]{2,1,0:T(8,128)(2,1)S(1)}, u32[]{:S(2)}, u32[]{:S(2)}) async-start(bf16[32,8,512]{2,1,0:T(8,128)(2,1)} %fusion.89), calls=%async_computation.1 | async-start | bytes 524288 | tf_op jit(solution)/shard_map/all_to_all | solution.py:35
  64.9 10.2 %all-to-all-done.1 = bf16[32,8,512]{2,1,0:T(8,128)(2,1)S(1)} async-done(((bf16[32,8,512]{2,1,0:T(8,128)(2,1)}), bf16[32,8,512]{2,1,0:T(8,128)(2,1)S(1)}, u32[]{:S(2)}, u32[]{:S(2)}) %all-to-all-start.1) | async-done | bytes 262176 | tf_op jit(solution)/shard_map/all_to_all | solution.py:35
  75.2 7.1 %while.38 = (s32[]{:T(128)}, f32[256,512]{1,0:T(8,128)S(1)}, s32[]{:T(128)}, s32[2048]{0:T(1024)S(1)}, bf16[2048,512]{0,1:T(8,128)(2,1)}, /*index=5*/s32[2048]{0...) while((s32[]{:T(128)}, f32[256,512]{1,0:T(8,128)S(1)}, ...), condition=%wide.region_10.11_spmd, body=%wide.region_7.10_spmd.sunk | while | flops 1619788288 | bytes 11829447 | solution.py:76
  75.7 1.3 convolution_convert_fusion.20
  77.0 1.1 constant_dynamic-slice_fusion.12
  78.3 3.2 %fusion.228 = (f32[512]{0:T(512)S(1)}, f32[512,512]{0,1:T(8,128)S(1)}) fusion(bf16[512,512]{1,0:T(8,128)(2,1)} %get-tuple-element.776, bf16[1536,512]{1,0:T(8,128)(2,1)} %get-tuple-element.775, bf16[512,512]{1,0:T(8,128)(2,1)S(1)} %convolution_convert_fusion.19, bf16[512,512]{1,0:T(8,128)(2,1)} %convolution_convert_fusion.20, ...), kind=kOutput, calls=%fused_computation.181.clone.1 | convolution fusion | flops 1080032768 | bytes 4720640 | tf_op jit(solution)/shard_map/while/body/dot_general | solution.py:20
  82.3 2.2 %fusion.154 = (f32[256]{0:T(256)S(1)}, f32[256,512]{1,0:T(8,128)S(1)}) fusion(bf16[2,512,512]{2,1,0:T(8,128)(2,1)} %param.35, bf16[2,1024,512]{2,1,0:T(8,128)(2,1)} %param.34, bf16[256,512]{1,0:T(8,128)(2,1)S(1)} %convert_element_type.211, bf16[256,512]{1,0:T(8,128)(2,1)S(1)} %get-tuple-element.823), kind=kOutput, calls=%fused_computation.189 | convolution fusion | flops 404487936 | bytes 2622464 | tf_op jit(solution)/shard_map/dot_general | solution.py:20
  85.8 23.8 %all-to-all-start.2 = ((bf16[32,4,512]{2,1,0:T(4,128)(2,1)}), bf16[32,4,512]{2,1,0:T(4,128)(2,1)}, u32[]{:S(2)}, u32[]{:S(2)}) async-start(bf16[32,4,512]{2,1,0:T(4,128)(2,1)} %reshape.177), calls=%async_computation.2 | async-start | bytes 262144 | tf_op jit(solution)/shard_map/all_to_all | solution.py:39
  110.6 3.2 %copy.33 = bf16[3,1024,512]{1,2,0:T(8,128)(2,1)S(1)} copy(bf16[3,1024,512]{2,1,0:T(8,128)(2,1)} %bitcast.126) | data formatting | bytes 6291456 | tf_op jit(solution)/shard_map/while | solution.py:128
  113.9 3.3 %all-to-all-done.2 = bf16[32,4,512]{2,1,0:T(4,128)(2,1)} async-done(((bf16[32,4,512]{2,1,0:T(4,128)(2,1)}), bf16[32,4,512]{2,1,0:T(4,128)(2,1)}, u32[]{:S(2)}, u32[]{:S(2)}) %all-to-all-start.2) | async-done | bytes 131104 | tf_op jit(solution)/shard_map/all_to_all | solution.py:39
  118.2 94.6 %while.39 = (s32[]{:T(128)}, bf16[1024,512]{1,0:T(8,128)(2,1)}, bf16[1024,512]{1,0:T(8,128)(2,1)}, bf16[3,1024,512]{1,2,0:T(8,128)(2,1)S(1)}, s32[3,1024]{1,0:T(...) while((s32[]{:T(128)}, bf16[1024,512]{1,0:T(8,128)(2,1)}, ...), condition=%wide.region_22.23_spmd, body=%wide.region_13.22_spmd.sunk | while | flops 4259776512 | bytes 55036200 | solution.py:128
  118.2 1.9 constant_dynamic-slice_fusion.13
  120.1 2.1 copy.46
  122.2 1.2 convolution_convert_fusion.21
  123.4 1.3 fusion.242
  124.7 1.1 dynamic-slice_bitcast_fusion.5
  125.8 4.6 %fusion.243 = (f32[512]{0:T(512)S(1)}, f32[512,512]{0,1:T(8,128)}) fusion(bf16[512,512]{1,0:T(8,128)(2,1)} %get-tuple-element.816, bf16[1536,512]{1,0:T(8,128)(2,1)} %get-tuple-element.815, bf16[512,512]{0,1:T(8,128)(2,1)} %copy.46, bf16[512,512]{0,1:T(8,128)(2,1)} %convolution_convert_fusion.21, bf16[512,512]{0,1:T(8,128)(2,1)} %get-tuple-element.681), kind=kOutput, calls=%fused_computation.184.clone.1 | convolution fusion | flops 1080032768 | bytes 4720640 | tf_op jit(solution)/shard_map/while/body/eval_jaxpr/dot_general | solution.py:20
  130.3 1.4 multiply_reduce_fusion.16
  131.7 2.2 %multiply_convert_fusion.22 = bf16[512,512]{0,1:T(8,128)(2,1)} fusion(f32[512,512]{0,1:T(8,128)} %get-tuple-element.682, f32[512]{0:T(512)S(1)} %add_rsqrt_fusion.16, f32[512]{0:T(512)S(1)} %broadcast_multiply_fusion.16), kind=kLoop, calls=%fused_computation.82.clone.1 | loop fusion | flops 786432 | bytes 1576960 | tf_op jit(solution)/shard_map/while/body/eval_jaxpr/convert_element_type | solution.py:118
  133.9 1.2 convolution_convert_fusion.22
  135.1 4.6 %fusion.244 = (f32[512]{0:T(512)S(1)}, f32[512,512]{0,1:T(8,128)}) fusion(bf16[512,512]{1,0:T(8,128)(2,1)} %get-tuple-element.816, bf16[1536,512]{1,0:T(8,128)(2,1)} %get-tuple-element.815, bf16[512,512]{0,1:T(8,128)(2,1)} %copy.46, bf16[512,512]{0,1:T(8,128)(2,1)} %convolution_convert_fusion.22, bf16[512,512]{0,1:T(8,128)(2,1)} %get-tuple-element.685), kind=kOutput, calls=%fused_computation.185.clone.1 | convolution fusion | flops 1080032768 | bytes 4720640 | tf_op jit(solution)/shard_map/while/body/eval_jaxpr/dot_general | solution.py:20
  139.7 1.5 multiply_reduce_fusion.17
  141.2 2.1 %multiply_convert_fusion.23 = bf16[512,512]{0,1:T(8,128)(2,1)} fusion(f32[512,512]{0,1:T(8,128)} %get-tuple-element.686, f32[512]{0:T(512)S(1)} %add_rsqrt_fusion.17, f32[512]{0:T(512)S(1)} %broadcast_multiply_fusion.17), kind=kLoop, calls=%fused_computation.85.clone.1 | loop fusion | flops 786432 | bytes 1576960 | tf_op jit(solution)/shard_map/while/body/eval_jaxpr/convert_element_type | solution.py:118
  143.3 1.2 convolution_convert_fusion.23
  145.4 4.5 %fusion.245 = (f32[512]{0:T(512)S(1)}, f32[512,512]{0,1:T(8,128)}) fusion(bf16[512,512]{1,0:T(8,128)(2,1)} %get-tuple-element.816, bf16[1536,512]{1,0:T(8,128)(2,1)} %get-tuple-element.815, bf16[512,512]{0,1:T(8,128)(2,1)} %copy.46, bf16[512,512]{0,1:T(8,128)(2,1)} %convolution_convert_fusion.23, bf16[512,512]{0,1:T(8,128)(2,1)} %dynamic-slice_bitcast_fusion.6), kind=kOutput, calls=%fused_computation.186.clone.1 | convolution fusion | flops 1080032768 | bytes 4720640 | tf_op jit(solution)/shard_map/while/body/eval_jaxpr/dot_general | solution.py:20
  150.0 1.5 multiply_reduce_fusion.18
  151.5 1.4 multiply_convert_fusion.24
  153.9 4.0 %fusion.246 = (f32[512]{0:T(512)S(1)}, f32[512,512]{0,1:T(8,128)}) fusion(bf16[512,512]{1,0:T(8,128)(2,1)} %get-tuple-element.818, bf16[1024,512]{1,0:T(8,128)(2,1)} %get-tuple-element.817, bf16[512,512]{0,1:T(8,128)(2,1)} %add_convert_fusion.7, bf16[512,512]{0,1:T(8,128)(2,1)} %copy.46), kind=kOutput, calls=%fused_computation.187.clone.1 | convolution fusion | flops 808975872 | bytes 3672064 | tf_op jit(solution)/shard_map/while/body/eval_jaxpr/dot_general | solution.py:20
  157.8 1.4 multiply_reduce_fusion.19
  159.2 2.4 %add_convert_fusion.8 = bf16[512,512]{0,1:T(8,128)(2,1)} fusion(bf16[512,512]{0,1:T(8,128)(2,1)} %copy.46, f32[512,512]{0,1:T(8,128)} %get-tuple-element.692, f32[512]{0:T(512)S(1)} %add_rsqrt_fusion.19, f32[512]{0:T(512)S(1)} %broadcast_multiply_fusion.19), kind=kLoop, calls=%fused_computation.78.clone.1 | loop fusion | flops 1310720 | bytes 2101248 | tf_op jit(solution)/shard_map/while/body/eval_jaxpr/convert_element_type | solution.py:125
  161.6 2.0 copy.47
  163.6 1.9 constant_dynamic-update-slice_fusion.2
  165.5 1.9 constant_dynamic-slice_fusion.13
  167.4 2.1 copy.46
  169.4 1.2 convolution_convert_fusion.21
  170.7 1.3 fusion.242
  172.0 1.1 dynamic-slice_bitcast_fusion.5
  173.0 4.6 %fusion.243 = (f32[512]{0:T(512)S(1)}, f32[512,512]{0,1:T(8,128)}) fusion(bf16[512,512]{1,0:T(8,128)(2,1)} %get-tuple-element.816, bf16[1536,512]{1,0:T(8,128)(2,1)} %get-tuple-element.815, bf16[512,512]{0,1:T(8,128)(2,1)} %copy.46, bf16[512,512]{0,1:T(8,128)(2,1)} %convolution_convert_fusion.21, bf16[512,512]{0,1:T(8,128)(2,1)} %get-tuple-element.681), kind=kOutput, calls=%fused_computation.184.clone.1 | convolution fusion | flops 1080032768 | bytes 4720640 | tf_op jit(solution)/shard_map/while/body/eval_jaxpr/dot_general | solution.py:20
  177.6 1.4 multiply_reduce_fusion.16
  179.0 2.2 %multiply_convert_fusion.22 = bf16[512,512]{0,1:T(8,128)(2,1)} fusion(f32[512,512]{0,1:T(8,128)} %get-tuple-element.682, f32[512]{0:T(512)S(1)} %add_rsqrt_fusion.16, f32[512]{0:T(512)S(1)} %broadcast_multiply_fusion.16), kind=kLoop, calls=%fused_computation.82.clone.1 | loop fusion | flops 786432 | bytes 1576960 | tf_op jit(solution)/shard_map/while/body/eval_jaxpr/convert_element_type | solution.py:118
  181.2 1.2 convolution_convert_fusion.22
  182.4 4.6 %fusion.244 = (f32[512]{0:T(512)S(1)}, f32[512,512]{0,1:T(8,128)}) fusion(bf16[512,512]{1,0:T(8,128)(2,1)} %get-tuple-element.816, bf16[1536,512]{1,0:T(8,128)(2,1)} %get-tuple-element.815, bf16[512,512]{0,1:T(8,128)(2,1)} %copy.46, bf16[512,512]{0,1:T(8,128)(2,1)} %convolution_convert_fusion.22, bf16[512,512]{0,1:T(8,128)(2,1)} %get-tuple-element.685), kind=kOutput, calls=%fused_computation.185.clone.1 | convolution fusion | flops 1080032768 | bytes 4720640 | tf_op jit(solution)/shard_map/while/body/eval_jaxpr/dot_general | solution.py:20
  187.0 1.5 multiply_reduce_fusion.17
  188.5 2.1 %multiply_convert_fusion.23 = bf16[512,512]{0,1:T(8,128)(2,1)} fusion(f32[512,512]{0,1:T(8,128)} %get-tuple-element.686, f32[512]{0:T(512)S(1)} %add_rsqrt_fusion.17, f32[512]{0:T(512)S(1)} %broadcast_multiply_fusion.17), kind=kLoop, calls=%fused_computation.85.clone.1 | loop fusion | flops 786432 | bytes 1576960 | tf_op jit(solution)/shard_map/while/body/eval_jaxpr/convert_element_type | solution.py:118
  190.6 1.2 convolution_convert_fusion.23
  192.7 4.5 %fusion.245 = (f32[512]{0:T(512)S(1)}, f32[512,512]{0,1:T(8,128)}) fusion(bf16[512,512]{1,0:T(8,128)(2,1)} %get-tuple-element.816, bf16[1536,512]{1,0:T(8,128)(2,1)} %get-tuple-element.815, bf16[512,512]{0,1:T(8,128)(2,1)} %copy.46, bf16[512,512]{0,1:T(8,128)(2,1)} %convolution_convert_fusion.23, bf16[512,512]{0,1:T(8,128)(2,1)} %dynamic-slice_bitcast_fusion.6), kind=kOutput, calls=%fused_computation.186.clone.1 | convolution fusion | flops 1080032768 | bytes 4720640 | tf_op jit(solution)/shard_map/while/body/eval_jaxpr/dot_general | solution.py:20
  197.3 1.5 multiply_reduce_fusion.18
  198.8 1.4 multiply_convert_fusion.24
  201.2 4.0 %fusion.246 = (f32[512]{0:T(512)S(1)}, f32[512,512]{0,1:T(8,128)}) fusion(bf16[512,512]{1,0:T(8,128)(2,1)} %get-tuple-element.818, bf16[1024,512]{1,0:T(8,128)(2,1)} %get-tuple-element.817, bf16[512,512]{0,1:T(8,128)(2,1)} %add_convert_fusion.7, bf16[512,512]{0,1:T(8,128)(2,1)} %copy.46), kind=kOutput, calls=%fused_computation.187.clone.1 | convolution fusion | flops 808975872 | bytes 3672064 | tf_op jit(solution)/shard_map/while/body/eval_jaxpr/dot_general | solution.py:20
  205.1 1.4 multiply_reduce_fusion.19
  206.5 2.4 %add_convert_fusion.8 = bf16[512,512]{0,1:T(8,128)(2,1)} fusion(bf16[512,512]{0,1:T(8,128)(2,1)} %copy.46, f32[512,512]{0,1:T(8,128)} %get-tuple-element.692, f32[512]{0:T(512)S(1)} %add_rsqrt_fusion.19, f32[512]{0:T(512)S(1)} %broadcast_multiply_fusion.19), kind=kLoop, calls=%fused_computation.78.clone.1 | loop fusion | flops 1310720 | bytes 2101248 | tf_op jit(solution)/shard_map/while/body/eval_jaxpr/convert_element_type | solution.py:125
  208.9 2.0 copy.47
  210.9 1.9 constant_dynamic-update-slice_fusion.2
  (96 shorter events, 13.8 us)
Async XLA Ops:
  3.4 18.3 %all-to-all-start = ((bf16[32,8,512]{2,1,0:T(8,128)(2,1)}), bf16[32,8,512]{2,1,0:T(8,128)(2,1)S(1)}, u32[]{:S(2)}, u32[]{:S(2)}) async-start(bf16[32,8,512]{2,1,0:T(8,128)(2,1)} %fusion.88), calls=%async_computation | async-start | bytes 524288 | tf_op jit(solution)/shard_map/all_to_all | solution.py:35
  12.7 4.1 %copy-start.5 = (bf16[2,512,512]{2,1,0:T(8,128)(2,1)S(1)}, bf16[2,512,512]{2,1,0:T(8,128)(2,1)}, u32[]{:S(2)}) copy-start(bf16[2,512,512]{2,1,0:T(8,128)(2,1)} %param.33) | copy-start | bytes 3145732
  17.9 3.8 %copy-start.3 = (bf16[256,512]{1,0:T(8,128)(2,1)S(1)}, bf16[256,512]{1,0:T(8,128)(2,1)}, u32[]{:S(2)}) copy-start(bf16[256,512]{1,0:T(8,128)(2,1)} %param.23) | copy-start | bytes 786436
  17.9 3.9 %copy-start.7 = (s32[2048]{0:T(1024)S(1)}, s32[2048]{0:T(1024)}, u32[]{:S(2)}) copy-start(s32[2048]{0:T(1024)} %param.28) | copy-start | bytes 24580
  17.9 3.9 %copy-start.8 = (s32[2048]{0:T(1024)S(1)}, s32[2048]{0:T(1024)}, u32[]{:S(2)}) copy-start(s32[2048]{0:T(1024)} %param.27) | copy-start | bytes 24580
  32.4 32.3 %copy-start.10 = (s32[1,32,4]{1,2,0:T(4,128)S(1)}, s32[1,32,4]{1,2,0:T(4,128)}, u32[]{:S(2)}) copy-start(s32[1,32,4]{1,2,0:T(4,128)} %param.30) | copy-start | bytes 1540
  33.8 41.3 %all-to-all-start.1 = ((bf16[32,8,512]{2,1,0:T(8,128)(2,1)}), bf16[32,8,512]{2,1,0:T(8,128)(2,1)S(1)}, u32[]{:S(2)}, u32[]{:S(2)}) async-start(bf16[32,8,512]{2,1,0:T(8,128)(2,1)} %fusion.89), calls=%async_computation.1 | async-start | bytes 524288 | tf_op jit(solution)/shard_map/all_to_all | solution.py:35
  84.5 25.2 %copy-start.4 = (bf16[32,32,512]{2,1,0:T(8,128)(2,1)S(1)}, bf16[32,32,512]{2,1,0:T(8,128)(2,1)}, u32[]{:S(2)}) copy-start(bf16[32,32,512]{2,1,0:T(8,128)(2,1)} %param.25) | copy-start | bytes 3145732
  84.9 28.9 %copy-start.6 = (bf16[256,512]{1,0:T(8,128)(2,1)}, bf16[256,512]{1,0:T(8,128)(2,1)S(1)}, u32[]{:S(2)}) copy-start(bf16[256,512]{1,0:T(8,128)(2,1)S(1)} %add_convert_fusion.3) | copy-start | bytes 786436
  85.8 31.4 %all-to-all-start.2 = ((bf16[32,4,512]{2,1,0:T(4,128)(2,1)}), bf16[32,4,512]{2,1,0:T(4,128)(2,1)}, u32[]{:S(2)}, u32[]{:S(2)}) async-start(bf16[32,4,512]{2,1,0:T(4,128)(2,1)} %reshape.177), calls=%async_computation.2 | async-start | bytes 262144 | tf_op jit(solution)/shard_map/all_to_all | solution.py:39
  110.6 3.2 %copy-start.9 = (s32[3,32,32]{2,1,0:T(8,128)S(1)}, s32[3,32,32]{2,1,0:T(8,128)}, u32[]{:S(2)}) copy-start(s32[3,32,32]{2,1,0:T(8,128)} %param.31) | copy-start | bytes 36868
  139.7 4.9 %copy-start = (bf16[1,1024,512]{1,2,0:T(8,128)(2,1)S(1)}, bf16[1,1024,512]{1,2,0:T(8,128)(2,1)}, u32[]{:S(2)}) copy-start(bf16[1,1024,512]{1,2,0:T(8,128)(2,1)} %get-tuple-element.689) | copy-start | bytes 3145732 | tf_op jit(solution)/shard_map/while
  150.0 2.8 %copy-start.1 = (bf16[512,512]{0,1:T(8,128)(2,1)S(1)}, bf16[512,512]{0,1:T(8,128)(2,1)}, u32[]{:S(2)}) copy-start(bf16[512,512]{0,1:T(8,128)(2,1)} %multiply_convert_fusion.22) | copy-start | bytes 1572868 | tf_op jit(solution)/shard_map/while
  150.0 2.9 %copy-start.2 = (bf16[512,512]{0,1:T(8,128)(2,1)S(1)}, bf16[512,512]{0,1:T(8,128)(2,1)}, u32[]{:S(2)}) copy-start(bf16[512,512]{0,1:T(8,128)(2,1)} %multiply_convert_fusion.23) | copy-start | bytes 1572868 | tf_op jit(solution)/shard_map/while
  187.0 4.9 %copy-start = (bf16[1,1024,512]{1,2,0:T(8,128)(2,1)S(1)}, bf16[1,1024,512]{1,2,0:T(8,128)(2,1)}, u32[]{:S(2)}) copy-start(bf16[1,1024,512]{1,2,0:T(8,128)(2,1)} %get-tuple-element.689) | copy-start | bytes 3145732 | tf_op jit(solution)/shard_map/while
  197.3 2.8 %copy-start.1 = (bf16[512,512]{0,1:T(8,128)(2,1)S(1)}, bf16[512,512]{0,1:T(8,128)(2,1)}, u32[]{:S(2)}) copy-start(bf16[512,512]{0,1:T(8,128)(2,1)} %multiply_convert_fusion.22) | copy-start | bytes 1572868 | tf_op jit(solution)/shard_map/while
  197.3 2.9 %copy-start.2 = (bf16[512,512]{0,1:T(8,128)(2,1)S(1)}, bf16[512,512]{0,1:T(8,128)(2,1)}, u32[]{:S(2)}) copy-start(bf16[512,512]{0,1:T(8,128)(2,1)} %multiply_convert_fusion.23) | copy-start | bytes 1572868 | tf_op jit(solution)/shard_map/while
where the time goes:
time: 214 us; the launch traced here: 213 us
  starting transfers between devices  62 us (29%)
  matrix products  61.2 us (29%)
  local copies, waits for them, and re-layouts  41 us (19%)
  other arithmetic  33.2 us (16%)
  waiting for transfers between devices  13.6 us (6%)
    dot_general x12, matrix products, perceptron(): jnp.dot(hidden, layer_two, preferred_element_type=jnp.float32)  46.1 us
    all_to_all x2, starting transfers between devices, mesh_route(): lax.all_to_all(outgoing, ('lat', 'lon'), split_axis=0, concat_axis=0, til...  38.2 us
    all_to_all x1, starting transfers between devices, decoder_route(): lax.all_to_all(outgoing, ('lat', 'lon'), split_axis=0, concat_axis=0, til...  23.8 us
    dot_general x13, matrix products, pick_rows(): jnp.dot(picker, lookup, preferred_element_type=jnp.float32)  14.1 us
    reduce_sum x12, other arithmetic, normalize(): spread = jnp.mean(centered * centered, axis=-1, keepdims=True)  12.1 us
    convert_element_type x6, other arithmetic, decode_advance(): result.astype(jnp.bfloat16)  11.3 us
    all_to_all x2, waiting for transfers between devices, mesh_route(): lax.all_to_all(outgoing, ('lat', 'lon'), split_axis=0, concat_axis=0, til...  10.2 us
    dynamic_slice x4, local copies, waits for them, and re-layouts, decode_advance(): grid_block = lax.dynamic_slice_in_dim(flat_grid, first_row, block_rows, 0)  7.83 us
  transfers between devices with their start and end apart: 3, of which 2 were waited for; matrix products, arithmetic and copies ran while one was open for 7% of the time, Pallas kernels for 0%

commit v1 on v0

v1 whole, which is shorter than its diff:
```python
import functools

import jax
import jax.numpy as jnp
from jax import lax
from jax.experimental import pallas as pl
from jax.experimental.pallas import tpu as pltpu
from jax.sharding import PartitionSpec as P

EPS = 1e-05
BF = jnp.bfloat16
F32 = jnp.float32
ROWS = 256
LANES = 128


def dot(a, b):
    return jnp.dot(a, b, preferred_element_type=F32)


def silu(v):
    half = 0.5 * v
    return half + half * jnp.tanh(half)


def normalize(values):
    average = jnp.mean(values, axis=-1, keepdims=True)
    centered = values - average
    spread = jnp.mean(centered * centered, axis=-1, keepdims=True)
    return centered * lax.rsqrt(spread + EPS)


def onehot(column, codes):
    return jnp.where(column == codes, 1.0, 0.0).astype(BF)


def kernel(
    dims,
    nodes_h, edges_h, grid_h, dedges_h,
    send_r, recv_r, halo_r, dlist_r, src_r,
    ef_h, es_h, nf_h, ns_h, df_h, ds_h, gf_h, gs_h,
    mesh_o, grid_o,
    nodes, edges, grid, dedges, ef, es, nf, ns, df, ds, gf, gs,
    index_a, index_h, index_d,
    pick, pick_t, dpick, table, dtable, early, early_grid, total,
    out0, out1, out2, in0, in1, in2,
    load_sem, send_sem, recv_sem, done_sem,
):
    n_lat, n_lon = dims
    count = n_lat * n_lon
    me = lax.axis_index("lat") * n_lon + lax.axis_index("lon")
    own, width = nodes.shape
    slots = edges.shape[0]
    layers = ef.shape[0]
    halo_slots = halo_r.shape[1]
    dec_slots = dlist_r.shape[1]
    cells = grid.shape[0]
    branches = src_r.shape[0]
    tile_rows, tile_cols = src_r.shape[1], src_r.shape[2]
    table_rows = own + count * halo_slots

    loads = []

    def load(src, dst):
        copy = pltpu.make_async_copy(src, dst, load_sem.at[len(loads)])
        loads.append(copy)
        copy.start()
        return copy

    def at(q):
        return (lax.div(q, n_lon), lax.rem(q, n_lon))

    l_nodes = load(nodes_h, nodes)
    l_ef = [load(ef_h.at[0], ef.at[0])]
    l_edges = load(edges_h, edges)
    l_es = [load(es_h.at[0], es.at[0])]
    l_nf = [load(nf_h.at[0], nf.at[0])]
    l_ns = [load(ns_h.at[0], ns.at[0])]

    barrier = pltpu.get_barrier_semaphore()

    @pl.loop(1, count)
    def _(step):
        pl.semaphore_signal(
            barrier, inc=1, device_id=at(lax.rem(me + step, count)),
            device_id_type=pl.DeviceIdType.MESH,
        )

    index_a[...] = jnp.zeros_like(index_a)
    index_h[...] = jnp.zeros_like(index_h)
    index_d[...] = jnp.zeros_like(index_d)
    groups = slots // LANES
    index_a[0:groups, :] = send_r[...]
    index_a[groups : 2 * groups, :] = recv_r[...]
    for b in range(branches):
        first = 2 * groups + b * tile_rows
        index_a[first : first + tile_rows, 0:tile_cols] = src_r[b]
    index_h[0:count, 0:halo_slots] = halo_r[...]
    index_d[0:count, 0:dec_slots] = dlist_r[...]
    index_d[0:count, dec_slots : 2 * dec_slots] = dlist_r[...]
    columns_a = jnp.transpose(index_a[...])
    columns_h = jnp.transpose(index_h[...])
    columns_d = jnp.transpose(index_d[...])

    def lists_pick(columns, per):
        rows = jnp.concatenate(
            [jnp.broadcast_to(columns[0:per, q : q + 1], (per, own)) for q in range(count)], axis=0
        )
        codes = lax.broadcasted_iota(jnp.int32, (per * count, own), 1)
        return jnp.where(rows == codes, 1.0, 0.0).astype(BF)

    halo_pick = lists_pick(columns_h, halo_slots)

    def post(outgoing, incoming, which):
        @pl.loop(1, count)
        def _(step):
            q = lax.rem(me + step, count)
            pltpu.make_async_remote_copy(
                src_ref=outgoing.at[q],
                dst_ref=incoming.at[me],
                send_sem=send_sem.at[which],
                recv_sem=recv_sem.at[which],
                device_id=at(q),
                device_id_type=pl.DeviceIdType.MESH,
            ).start()

        incoming[pl.ds(me, 1)] = outgoing[pl.ds(me, 1)]

    def drain(buffer, sem):
        whole = buffer.at[pl.ds(0, count - 1)]
        pltpu.make_async_copy(whole, whole, sem).wait()

    def halo_send(outgoing, incoming, which):
        chosen = dot(halo_pick, nodes[...])
        outgoing[...] = chosen.reshape(count, halo_slots, width).astype(BF)
        if which == 0:
            pl.semaphore_wait(barrier, count - 1)
        post(outgoing, incoming, which)

    l_nodes.wait()
    halo_send(out0, in0, 0)

    l_ef += [load(ef_h.at[l], ef.at[l]) for l in range(1, layers)]
    l_es += [load(es_h.at[l], es.at[l]) for l in range(1, layers)]
    l_nf += [load(nf_h.at[l], nf.at[l]) for l in range(1, layers)]
    l_ns += [load(ns_h.at[l], ns.at[l]) for l in range(1, layers)]
    l_df = load(df_h, df)
    l_grid = load(grid_h, grid)
    l_dedges = load(dedges_h, dedges)
    l_gf = load(gf_h, gf)
    l_ds = load(ds_h, ds)
    l_gs = load(gs_h, gs)

    def rows_of(step):
        return pl.ds(pl.multiple_of(step * ROWS, ROWS), ROWS)

    send_codes = lax.broadcasted_iota(jnp.int32, (LANES, table_rows), 1)
    recv_codes = lax.broadcasted_iota(jnp.int32, (LANES, own), 1)
    node_codes = lax.broadcasted_iota(jnp.int32, (own, LANES), 0)
    for g in range(groups):
        span = slice(g * LANES, (g + 1) * LANES)
        pick[span, 0:table_rows] = onehot(columns_a[:, g : g + 1], send_codes)
        pick[span, table_rows:] = onehot(columns_a[:, groups + g : groups + g + 1], recv_codes)
        pick_t[:, span] = jnp.where(recv_r[g : g + 1, :] == node_codes, 1.0, 0.0).astype(BF)

    outs, ins = [out0, out1], [in0, in1]
    for l in range(layers):
        l_ef[l].wait()
        if l == 0:
            l_edges.wait()
        table[0:own, :] = dot(nodes[...], ef[l, width : 2 * width, :]).astype(BF)
        table[table_rows:, :] = dot(nodes[...], ef[l, 2 * width :, :]).astype(BF)

        @pl.loop(0, slots // ROWS)
        def _(step):
            rows = rows_of(step)
            early[rows, :] = dot(edges[rows, :], ef[l, 0:width, :])

        if l == 1 or layers == 1:
            point_codes = lax.broadcasted_iota(jnp.int32, (tile_cols, 2 * dec_slots * count), 1)
            point_codes = (point_codes // (2 * dec_slots)) * dec_slots + point_codes % dec_slots
            for b in range(branches):
                for r in range(tile_rows):
                    lane = 2 * groups + b * tile_rows + r
                    first = b * cells + r * tile_cols
                    dpick[first : first + tile_cols, :] = onehot(
                        columns_a[0:tile_cols, lane : lane + 1], point_codes
                    )

        drain(ins[l], recv_sem.at[l])
        far = ins[l][...].astype(F32).reshape(count * halo_slots, width).astype(BF)
        table[own:table_rows, :] = dot(far, ef[l, width : 2 * width, :]).astype(BF)
        total[...] = jnp.zeros_like(total)
        l_es[l].wait()

        @pl.loop(0, slots // ROWS)
        def _(step):
            rows = rows_of(step)
            hidden = silu(early[rows, :] + dot(pick[rows, :], table[...])).astype(BF)
            result = normalize(dot(hidden, es[l]))
            total[...] += dot(pick_t[:, rows], result.astype(BF))
            if l < layers - 1:
                edges[rows, :] = (edges[rows, :].astype(F32) + result).astype(BF)

        l_nf[l].wait()
        l_ns[l].wait()
        hidden = silu(
            dot(nodes[...], nf[l, 0:width, :]) + dot(total[...].astype(BF), nf[l, width:, :])
        ).astype(BF)
        result = normalize(dot(hidden, ns[l]))
        nodes[...] = (nodes[...].astype(F32) + result).astype(BF)
        if l < layers - 1:
            halo_send(outs[l + 1], ins[l + 1], l + 1)

    half = width // 2
    chosen = dot(lists_pick(columns_d, 2 * dec_slots), nodes[...])
    place = lax.broadcasted_iota(jnp.int32, (2 * dec_slots * count, half), 0)
    upper = (place % (2 * dec_slots)) >= dec_slots
    chosen = jnp.where(upper, chosen[:, half:], chosen[:, :half])
    out2[...] = chosen.reshape(count, 2 * dec_slots, half).astype(BF)
    post(out2, in2, layers)
    mesh_copy = pltpu.make_async_copy(nodes, mesh_o, done_sem.at[0])
    mesh_copy.start()

    l_df.wait()
    l_grid.wait()
    l_dedges.wait()
    l_gf.wait()
    steps = cells // ROWS

    @pl.loop(0, steps)
    def _(step):
        rows = rows_of(step)
        here = grid[rows, :]
        shared = dot(here, df[2 * width :, :])
        for b in range(branches):
            span = pl.ds(pl.multiple_of(b * cells + step * ROWS, ROWS), ROWS)
            early[span, :] = shared + dot(dedges[span, :], df[0:width, :])
        early_grid[rows, :] = dot(here, gf[0:width, :])

    l_ds.wait()
    l_gs.wait()
    drain(in2, recv_sem.at[layers])
    far = in2[...].astype(F32).reshape(count * 2 * dec_slots, half).astype(BF)
    place = lax.broadcasted_iota(jnp.int32, (2 * dec_slots * count, width), 0)
    upper = (place % (2 * dec_slots)) >= dec_slots
    dtable[...] = jnp.where(
        upper, dot(far, df[width + half : 2 * width, :]), dot(far, df[width : width + half, :])
    ).astype(BF)

    @pl.loop(0, steps)
    def _(step):
        rows = rows_of(step)
        summed = None
        for b in range(branches):
            span = pl.ds(pl.multiple_of(b * cells + step * ROWS, ROWS), ROWS)
            hidden = silu(early[span, :] + dot(dpick[span, :], dtable[...])).astype(BF)
            result = normalize(dot(hidden, ds[...])).astype(BF).astype(F32)
            summed = result if summed is None else summed + result
        hidden = silu(early_grid[rows, :] + dot(summed.astype(BF), gf[width:, :])).astype(BF)
        result = normalize(dot(hidden, gs[...]))
        grid[rows, :] = (grid[rows, :].astype(F32) + result).astype(BF)
        pltpu.make_async_copy(grid.at[rows], grid_o.at[rows], done_sem.at[1 + step]).start()

    for b, buffer in enumerate([out0, out1, out2]):
        drain(buffer, send_sem.at[b])
    mesh_copy.wait()

    @pl.loop(0, steps)
    def _(step):
        rows = rows_of(step)
        pltpu.make_async_copy(grid.at[rows], grid_o.at[rows], done_sem.at[1 + step]).wait()


def shards(
    dims,
    mesh_nodes, mesh_edges, grid_state, decoder_edges, edge_send, edge_recv, halo_lists,
    decoder_lists, decoder_sources, edge_first, edge_second, node_first, node_second,
    decoder_first, decoder_second, grid_first, grid_second,
):
    own, width = mesh_nodes.shape
    slots = mesh_edges.shape[0]
    tile_lat, tile_lon = grid_state.shape[0], grid_state.shape[1]
    cells = tile_lat * tile_lon
    branches = decoder_edges.shape[0]
    count, halo_slots = halo_lists.shape[1], halo_lists.shape[2]
    dec_slots = decoder_lists.shape[2]
    layers = edge_first.shape[0]
    table_rows = own + count * halo_slots
    list_rows = -(-count // LANES) * LANES
    index_rows = -(-(2 * slots // LANES + branches * tile_lat) // LANES) * LANES
    hbm = pl.BlockSpec(memory_space=pl.ANY)
    vmem = pl.BlockSpec(memory_space=pltpu.VMEM)

    big = [mesh_nodes, mesh_edges, grid_state.reshape(cells, width),
           decoder_edges.reshape(branches * cells, width)]
    weights = [edge_first, edge_second, node_first, node_second,
               decoder_first, decoder_second, grid_first, grid_second]
    small = [edge_send.reshape(-1, LANES), edge_recv.reshape(-1, LANES), halo_lists[0],
             decoder_lists[0], decoder_sources]

    held = [pltpu.VMEM(a.shape, a.dtype) for a in big + weights]
    scratch = held + [
        pltpu.VMEM((index_rows, LANES), jnp.int32),
        pltpu.VMEM((list_rows, LANES), jnp.int32),
        pltpu.VMEM((list_rows, LANES), jnp.int32),
        pltpu.VMEM((slots, table_rows + own), BF),
        pltpu.VMEM((own, slots), BF),
        pltpu.VMEM((branches * cells, 2 * dec_slots * count), BF),
        pltpu.VMEM((table_rows + own, width), BF),
        pltpu.VMEM((2 * dec_slots * count, width), BF),
        pltpu.VMEM((max(slots, branches * cells), width), F32),
        pltpu.VMEM((cells, width), F32),
        pltpu.VMEM((own, width), F32),
        pltpu.VMEM((count, halo_slots, width), BF),
        pltpu.VMEM((count, halo_slots, width), BF),
        pltpu.VMEM((count, 2 * dec_slots, width // 2), BF),
        pltpu.VMEM((count, halo_slots, width), BF),
        pltpu.VMEM((count, halo_slots, width), BF),
        pltpu.VMEM((count, 2 * dec_slots, width // 2), BF),
        pltpu.SemaphoreType.DMA((8 + 4 * layers,)),
        pltpu.SemaphoreType.DMA((layers + 1,)),
        pltpu.SemaphoreType.DMA((layers + 1,)),
        pltpu.SemaphoreType.DMA((1 + cells // ROWS,)),
    ]
    mesh_final, grid_final = pl.pallas_call(
        functools.partial(kernel, dims),
        out_shape=(
            jax.ShapeDtypeStruct((own, width), BF),
            jax.ShapeDtypeStruct((cells, width), BF),
        ),
        in_specs=[hbm] * len(big) + [vmem] * len(small) + [hbm] * len(weights),
        out_specs=(hbm, hbm),
        scratch_shapes=scratch,
        compiler_params=pltpu.CompilerParams(
            collective_id=0, has_side_effects=True, vmem_limit_bytes=60 * 1024 * 1024
        ),
        name="processor",
    )(*big, *small, *weights)
    return mesh_final, grid_final.reshape(tile_lat, tile_lon, width)


def solution(mesh):
    both = ("lat", "lon")
    placed = (
        P(both, None),
        P(both, None),
        P("lat", "lon", None),
        P(None, "lat", "lon", None),
        P(both),
        P(both),
        P(both, None, None),
        P(both, None, None),
        P(None, "lat", "lon"),
    ) + (P(),) * 8
    dims = (mesh.shape["lat"], mesh.shape["lon"])
    return jax.shard_map(
        functools.partial(shards, dims),
        mesh=mesh,
        in_specs=placed,
        out_specs=(P(both, None), P("lat", "lon", None)),
        check_vma=False,
    )
```

time: 214 us -> 63.4 us (0.30)
  starting transfers between devices: 62 us -> 0 us
  matrix products: 61.2 us -> 0 us
  Pallas kernels: 0 us -> 55.8 us
  local copies, waits for them, and re-layouts: 41 us -> 6.71 us
  other arithmetic: 33.2 us -> 0 us
  waiting for transfers between devices: 13.6 us -> 0 us
    all_to_all x3 -> x0, starting transfers between devices: 62 us -> none  [the longest x2 38.2 us: mesh_route(): lax.all_to_all(outgoing, ('lat', 'lon'), split_axis=0, concat_axis=0, til...]
    dot_general x27 -> x0, matrix products: 61.2 us -> none  [the longest x12 46.1 us: perceptron(): jnp.dot(hidden, layer_two, preferred_element_type=jnp.float32)]
    pallas_call x0 -> x1, Pallas kernels: none -> 55.8 us  [shards(): pl.pallas_call(functools.partial(kernel, dims), out_shape=(jax.ShapeDtype...]
    convert_element_type x14 -> x0, other arithmetic: 18.5 us -> none  [the longest x6 11.3 us: decode_advance(): result.astype(jnp.bfloat16)]
    dynamic_slice x20 -> x0, local copies, waits for them, and re-layouts: 14.6 us -> none  [the longest x4 7.83 us: decode_advance(): grid_block = lax.dynamic_slice_in_dim(flat_grid, first_row, block_rows, 0)]
    all_to_all x3 -> x0, waiting for transfers between devices: 13.6 us -> none  [the longest x2 10.2 us: mesh_route(): lax.all_to_all(outgoing, ('lat', 'lon'), split_axis=0, concat_axis=0, til...]
    reduce_sum x13 -> x0, other arithmetic: 13.4 us -> none  [the longest x12 12.1 us: normalize(): spread = jnp.mean(centered * centered, axis=-1, keepdims=True)]
    dynamic_update_slice x4 -> x0, local copies, waits for them, and re-layouts: 7.82 us -> none  [decode_advance(): return lax.dynamic_update_slice_in_dim(updated, fresh, first_row, 0)]
  transfers between devices with their start and end apart: 3 -> 0, of which waited for: 2 -> 0; matrix products, arithmetic and copies ran while one was open for 7% -> 0% of each run, Pallas kernels for 0% -> 0%
where the time goes in v1:
time: 63.4 us; the launch traced here: 63.1 us
  Pallas kernels  55.8 us (88%)
  local copies, waits for them, and re-layouts  6.71 us (11%)
  between operations  0.64 us (1%)
    pallas_call x1, Pallas kernels, shards(): pl.pallas_call(functools.partial(kernel, dims), out_shape=(jax.ShapeDtype...  55.8 us
    unnamed x3, local copies, waits for them, and re-layouts  5.34 us
    squeeze x1, local copies, waits for them, and re-layouts, shards(): decoder_lists[0]  1.37 us

profile of v1, /device:TPU:0, one launch (start us, length us, event | category | flops | bytes accessed | tf_op | source)
XLA Modules:
  0.0 63.1 jit_solution(4448582587896342920)
XLA Ops:
  0.6 1.4 %copy.19 = s32[1,32,8]{2,1,0:T(8,128)} copy(s32[1,32,8]{1,2,0:T(8,128)} %param.23) | data formatting | bytes 2048 | tf_op args[6]
  2.0 1.4 %copy.20.dlist_r = s32[32,4]{1,0:T(8,128)} copy(s32[32,4]{0,1:T(4,128)} %bitcast.13) | data formatting | bytes 1024 | tf_op jit(solution)/shard_map/squeeze | solution.py:300
  3.4 55.8 %processor.1 = (bf16[256,512]{1,0:T(8,128)(2,1)}, bf16[1024,512]{1,0:T(8,128)(2,1)}) custom-call(bf16[256,512]{1,0:T(8,128)(2,1)} %nodes_h.1, bf16[2048,512]{1,0:T(8,128)(2,1)} %edges_h.1, bf16[1024,512]{1,0:T(8,128)(2,1)} %bitcast.8, bf16[3072,512]{1,0:T(8,128)(2,1)} %bitcast.7, s32[16,128]{1,0:T(8,128)} %bitcast.11, s32[16,128]{1,0:T(8,128)} %bitcast.12, ...), custom_call_target="tpu_custom_call" | custom-call | tf_op jit(solution)/shard_map/processor/pallas_call | solution.py:326
  59.1 1.7 %copy.23 = bf16[256,512]{1,0:T(8,128)(2,1)} copy(bf16[256,512]{1,0:T(8,128)(2,1)} %get-tuple-element.8) | data formatting | bytes 524288
  60.8 2.3 %copy.24 = bf16[32,32,512]{2,1,0:T(8,128)(2,1)} copy(bf16[32,32,512]{2,1,0:T(8,128)(2,1)} %bitcast.9) | data formatting | bytes 2097152

commit v2 on v1

--- a/solution.py
+++ b/solution.py
@@ -18,20 +18,37 @@
     return jnp.dot(a, b, preferred_element_type=F32)
 
 
-def silu(v):
-    half = 0.5 * v
+def silu(half):
+    half = half.astype(BF)
     return half + half * jnp.tanh(half)
 
 
-def normalize(values):
-    average = jnp.mean(values, axis=-1, keepdims=True)
-    centered = values - average
+def normalize(centered):
     spread = jnp.mean(centered * centered, axis=-1, keepdims=True)
     return centered * lax.rsqrt(spread + EPS)
 
 
-def onehot(column, codes):
-    return jnp.where(column == codes, 1.0, 0.0).astype(BF)
+def center(ref):
+    values = ref[...].astype(F32)
+    ref[...] = (values - jnp.mean(values, axis=-1, keepdims=True)).astype(BF)
+
+
+def onehot(indices, codes):
+    return jnp.where(indices == codes, BF(1), BF(0))
+
+
+def lane_codes(rows):
+    return lax.broadcasted_iota(jnp.int32, (rows, LANES), 1)
+
+
+def fill(ref, rows, first, columns, codes, blocks, base):
+    shape = codes.shape
+    wide = [jnp.broadcast_to(column, shape) for column in columns]
+    for k in range(blocks):
+        low = first + k * LANES
+        j = base * k // 256
+        near = codes + BF(base * k - 256 * j)
+        ref[rows, low : low + LANES] = onehot(wide[j], near)
 
 
 def kernel(
@@ -41,7 +58,7 @@
     ef_h, es_h, nf_h, ns_h, df_h, ds_h, gf_h, gs_h,
     mesh_o, grid_o,
     nodes, edges, grid, dedges, ef, es, nf, ns, df, ds, gf, gs,
-    index_a, index_h, index_d,
+    index_a, index_d,
     pick, pick_t, dpick, table, dtable, early, early_grid, total,
     out0, out1, out2, in0, in1, in2,
     load_sem, send_sem, recv_sem, done_sem,
@@ -52,8 +69,8 @@
     own, width = nodes.shape
     slots = edges.shape[0]
     layers = ef.shape[0]
-    halo_slots = halo_r.shape[1]
-    dec_slots = dlist_r.shape[1]
+    halo_slots = halo_r.shape[0]
+    dec_slots = dlist_r.shape[0]
     cells = grid.shape[0]
     branches = src_r.shape[0]
     tile_rows, tile_cols = src_r.shape[1], src_r.shape[2]
@@ -87,20 +104,14 @@
         )
 
     index_a[...] = jnp.zeros_like(index_a)
-    index_h[...] = jnp.zeros_like(index_h)
-    index_d[...] = jnp.zeros_like(index_d)
     groups = slots // LANES
     index_a[0:groups, :] = send_r[...]
     index_a[groups : 2 * groups, :] = recv_r[...]
     for b in range(branches):
         first = 2 * groups + b * tile_rows
         index_a[first : first + tile_rows, 0:tile_cols] = src_r[b]
-    index_h[0:count, 0:halo_slots] = halo_r[...]
-    index_d[0:count, 0:dec_slots] = dlist_r[...]
-    index_d[0:count, dec_slots : 2 * dec_slots] = dlist_r[...]
-    columns_a = jnp.transpose(index_a[...])
-    columns_h = jnp.transpose(index_h[...])
-    columns_d = jnp.transpose(index_d[...])
+    index_d[0:dec_slots, :] = dlist_r[...]
+    index_d[dec_slots : 2 * dec_slots, :] = dlist_r[...]
 
     def lists_pick(columns, per):
         rows = jnp.concatenate(
@@ -109,7 +120,7 @@
         codes = lax.broadcasted_iota(jnp.int32, (per * count, own), 1)
         return jnp.where(rows == codes, 1.0, 0.0).astype(BF)
 
-    halo_pick = lists_pick(columns_h, halo_slots)
+    halo_pick = lists_pick(halo_r[...], halo_slots)
 
     def post(outgoing, incoming, which):
         @pl.loop(1, count)
@@ -154,66 +165,82 @@
     def rows_of(step):
         return pl.ds(pl.multiple_of(step * ROWS, ROWS), ROWS)
 
-    send_codes = lax.broadcasted_iota(jnp.int32, (LANES, table_rows), 1)
-    recv_codes = lax.broadcasted_iota(jnp.int32, (LANES, own), 1)
-    node_codes = lax.broadcasted_iota(jnp.int32, (own, LANES), 0)
+    columns_a = jnp.transpose(index_a[...]).astype(F32)
+    shifted = [(columns_a - 256.0 * j).astype(BF) for j in range(-(-table_rows // 256))]
+    row_codes = lane_codes(LANES).astype(F32).astype(BF)
+    node_codes = lax.broadcasted_iota(jnp.int32, (own, LANES), 0).astype(F32).astype(BF)
     for g in range(groups):
         span = slice(g * LANES, (g + 1) * LANES)
-        pick[span, 0:table_rows] = onehot(columns_a[:, g : g + 1], send_codes)
-        pick[span, table_rows:] = onehot(columns_a[:, groups + g : groups + g + 1], recv_codes)
-        pick_t[:, span] = jnp.where(recv_r[g : g + 1, :] == node_codes, 1.0, 0.0).astype(BF)
+        lane, other = slice(g, g + 1), slice(groups + g, groups + g + 1)
+        fill(pick, span, 0, [c[:, lane] for c in shifted], row_codes, table_rows // LANES, LANES)
+        fill(pick, span, table_rows, [c[:, other] for c in shifted[: -(-own // 256)]],
+             row_codes, own // LANES, LANES)
+        targets = jnp.broadcast_to(recv_r[g : g + 1, :].astype(F32).astype(BF), (own, LANES))
+        pick_t[:, span] = onehot(targets, node_codes)
 
     outs, ins = [out0, out1], [in0, in1]
     for l in range(layers):
         l_ef[l].wait()
         if l == 0:
             l_edges.wait()
-        table[0:own, :] = dot(nodes[...], ef[l, width : 2 * width, :]).astype(BF)
-        table[table_rows:, :] = dot(nodes[...], ef[l, 2 * width :, :]).astype(BF)
+        table[0:own, :] = (0.5 * dot(nodes[...], ef[l, width : 2 * width, :])).astype(BF)
+        table[table_rows:, :] = (0.5 * dot(nodes[...], ef[l, 2 * width :, :])).astype(BF)
 
         @pl.loop(0, slots // ROWS)
         def _(step):
             rows = rows_of(step)
-            early[rows, :] = dot(edges[rows, :], ef[l, 0:width, :])
+            early[rows, :] = 0.5 * dot(edges[rows, :], ef[l, 0:width, :])
+
+        l_nf[l].wait()
+        early_grid[0:own, :] = 0.5 * dot(nodes[...], nf[l, 0:width, :])
+        l_es[l].wait()
+        l_ns[l].wait()
+        center(es.at[l])
+        center(ns.at[l])
 
         if l == 1 or layers == 1:
-            point_codes = lax.broadcasted_iota(jnp.int32, (tile_cols, 2 * dec_slots * count), 1)
-            point_codes = (point_codes // (2 * dec_slots)) * dec_slots + point_codes % dec_slots
+            l_ds.wait()
+            l_gs.wait()
+            l_gf.wait()
+            center(ds)
+            center(gs)
+            gf[width:, :] = gf[width:, :] * BF(0.5)
+            codes = lane_codes(tile_cols)
+            codes = (codes // (2 * dec_slots)) * dec_slots + codes % dec_slots
+            codes = codes.astype(F32).astype(BF)
+            needed = -(-dec_slots * count // 256)
             for b in range(branches):
                 for r in range(tile_rows):
                     lane = 2 * groups + b * tile_rows + r
                     first = b * cells + r * tile_cols
-                    dpick[first : first + tile_cols, :] = onehot(
-                        columns_a[0:tile_cols, lane : lane + 1], point_codes
-                    )
+                    fill(dpick, slice(first, first + tile_cols), 0,
+                         [c[0:tile_cols, lane : lane + 1] for c in shifted[:needed]],
+                         codes, 2 * dec_slots * count // LANES, LANES // 2)
 
         drain(ins[l], recv_sem.at[l])
         far = ins[l][...].astype(F32).reshape(count * halo_slots, width).astype(BF)
-        table[own:table_rows, :] = dot(far, ef[l, width : 2 * width, :]).astype(BF)
+        table[own:table_rows, :] = (0.5 * dot(far, ef[l, width : 2 * width, :])).astype(BF)
         total[...] = jnp.zeros_like(total)
-        l_es[l].wait()
 
         @pl.loop(0, slots // ROWS)
         def _(step):
             rows = rows_of(step)
-            hidden = silu(early[rows, :] + dot(pick[rows, :], table[...])).astype(BF)
+            hidden = silu(early[rows, :] + dot(pick[rows, :], table[...]))
             result = normalize(dot(hidden, es[l]))
             total[...] += dot(pick_t[:, rows], result.astype(BF))
             if l < layers - 1:
                 edges[rows, :] = (edges[rows, :].astype(F32) + result).astype(BF)
 
-        l_nf[l].wait()
-        l_ns[l].wait()
         hidden = silu(
-            dot(nodes[...], nf[l, 0:width, :]) + dot(total[...].astype(BF), nf[l, width:, :])
-        ).astype(BF)
+            early_grid[0:own, :] + 0.5 * dot(total[...].astype(BF), nf[l, width:, :])
+        )
         result = normalize(dot(hidden, ns[l]))
         nodes[...] = (nodes[...].astype(F32) + result).astype(BF)
         if l < layers - 1:
             halo_send(outs[l + 1], ins[l + 1], l + 1)
 
     half = width // 2
-    chosen = dot(lists_pick(columns_d, 2 * dec_slots), nodes[...])
+    chosen = dot(lists_pick(index_d[...], 2 * dec_slots), nodes[...])
     place = lax.broadcasted_iota(jnp.int32, (2 * dec_slots * count, half), 0)
     upper = (place % (2 * dec_slots)) >= dec_slots
     chosen = jnp.where(upper, chosen[:, half:], chosen[:, :half])
@@ -225,28 +252,26 @@
     l_df.wait()
     l_grid.wait()
     l_dedges.wait()
-    l_gf.wait()
     steps = cells // ROWS
 
     @pl.loop(0, steps)
     def _(step):
         rows = rows_of(step)
         here = grid[rows, :]
-        shared = dot(here, df[2 * width :, :])
+        shared = 0.5 * dot(here, df[2 * width :, :])
         for b in range(branches):
             span = pl.ds(pl.multiple_of(b * cells + step * ROWS, ROWS), ROWS)
-            early[span, :] = shared + dot(dedges[span, :], df[0:width, :])
-        early_grid[rows, :] = dot(here, gf[0:width, :])
-
-    l_ds.wait()
-    l_gs.wait()
+            early[span, :] = shared + 0.5 * dot(dedges[span, :], df[0:width, :])
+        early_grid[rows, :] = 0.5 * dot(here, gf[0:width, :])
+
     drain(in2, recv_sem.at[layers])
     far = in2[...].astype(F32).reshape(count * 2 * dec_slots, half).astype(BF)
     place = lax.broadcasted_iota(jnp.int32, (2 * dec_slots * count, width), 0)
     upper = (place % (2 * dec_slots)) >= dec_slots
-    dtable[...] = jnp.where(
+    chosen = jnp.where(
         upper, dot(far, df[width + half : 2 * width, :]), dot(far, df[width : width + half, :])
-    ).astype(BF)
+    )
+    dtable[...] = (0.5 * chosen).astype(BF)
 
     @pl.loop(0, steps)
     def _(step):
@@ -254,10 +279,10 @@
         summed = None
         for b in range(branches):
             span = pl.ds(pl.multiple_of(b * cells + step * ROWS, ROWS), ROWS)
-            hidden = silu(early[span, :] + dot(dpick[span, :], dtable[...])).astype(BF)
+            hidden = silu(early[span, :] + dot(dpick[span, :], dtable[...]))
             result = normalize(dot(hidden, ds[...])).astype(BF).astype(F32)
             summed = result if summed is None else summed + result
-        hidden = silu(early_grid[rows, :] + dot(summed.astype(BF), gf[width:, :])).astype(BF)
+        hidden = silu(early_grid[rows, :] + dot(summed.astype(BF), gf[width:, :]))
         result = normalize(dot(hidden, gs[...]))
         grid[rows, :] = (grid[rows, :].astype(F32) + result).astype(BF)
         pltpu.make_async_copy(grid.at[rows], grid_o.at[rows], done_sem.at[1 + step]).start()
@@ -287,7 +312,6 @@
     dec_slots = decoder_lists.shape[2]
     layers = edge_first.shape[0]
     table_rows = own + count * halo_slots
-    list_rows = -(-count // LANES) * LANES
     index_rows = -(-(2 * slots // LANES + branches * tile_lat) // LANES) * LANES
     hbm = pl.BlockSpec(memory_space=pl.ANY)
     vmem = pl.BlockSpec(memory_space=pltpu.VMEM)
@@ -296,21 +320,20 @@
            decoder_edges.reshape(branches * cells, width)]
     weights = [edge_first, edge_second, node_first, node_second,
                decoder_first, decoder_second, grid_first, grid_second]
-    small = [edge_send.reshape(-1, LANES), edge_recv.reshape(-1, LANES), halo_lists[0],
-             decoder_lists[0], decoder_sources]
+    small = [edge_send.reshape(-1, LANES), edge_recv.reshape(-1, LANES), halo_lists[0].T,
+             decoder_lists[0].T, decoder_sources]
 
     held = [pltpu.VMEM(a.shape, a.dtype) for a in big + weights]
     scratch = held + [
         pltpu.VMEM((index_rows, LANES), jnp.int32),
-        pltpu.VMEM((list_rows, LANES), jnp.int32),
-        pltpu.VMEM((list_rows, LANES), jnp.int32),
+        pltpu.VMEM((2 * dec_slots, count), jnp.int32),
         pltpu.VMEM((slots, table_rows + own), BF),
         pltpu.VMEM((own, slots), BF),
         pltpu.VMEM((branches * cells, 2 * dec_slots * count), BF),
         pltpu.VMEM((table_rows + own, width), BF),
         pltpu.VMEM((2 * dec_slots * count, width), BF),
         pltpu.VMEM((max(slots, branches * cells), width), F32),
-        pltpu.VMEM((cells, width), F32),
+        pltpu.VMEM((max(cells, own), width), F32),
         pltpu.VMEM((own, width), F32),
         pltpu.VMEM((count, halo_slots, width), BF),
         pltpu.VMEM((count, halo_slots, width), BF),

time: 63.4 us -> 57.7 us (0.910)
  Pallas kernels: 55.8 us -> 52.8 us
  local copies, waits for them, and re-layouts: 6.71 us -> 3.97 us
    pallas_call x1, Pallas kernels: 55.8 us -> 52.8 us  [shards(): pl.pallas_call(functools.partial(kernel, dims), out_shape=(jax.ShapeDtype...]
    unnamed x3 -> x2, local copies, waits for them, and re-layouts: 5.34 us -> 3.97 us
    squeeze x1 -> x0, local copies, waits for them, and re-layouts: 1.37 us -> none  [shards(): decoder_lists[0]]
where the time goes in v2:
time: 57.7 us; the launch traced here: 57.4 us
  Pallas kernels  52.8 us (92%)
  local copies, waits for them, and re-layouts  3.97 us (7%)
  between operations  0.65 us (1%)
    pallas_call x1, Pallas kernels, shards(): pl.pallas_call(functools.partial(kernel, dims), out_shape=(jax.ShapeDtype...  52.8 us
    unnamed x2, local copies, waits for them, and re-layouts  3.97 us

profile of v2, /device:TPU:0, one launch (start us, length us, event | category | flops | bytes accessed | tf_op | source)
XLA Modules:
  0.0 57.4 jit_solution(9334847323216902797)
XLA Ops:
  0.6 52.8 %processor.1 = (bf16[256,512]{1,0:T(8,128)(2,1)}, bf16[1024,512]{1,0:T(8,128)(2,1)}) custom-call(bf16[256,512]{1,0:T(8,128)(2,1)} %nodes_h.1, bf16[2048,512]{1,0:T(8,128)(2,1)} %edges_h.1, bf16[1024,512]{1,0:T(8,128)(2,1)} %bitcast.12, bf16[3072,512]{1,0:T(8,128)(2,1)} %bitcast.11, s32[16,128]{1,0:T(8,128)} %bitcast.14, s32[16,128]{1,0:T(8,128)} %bitcast.15, ...), custom_call_target="tpu_custom_call" | custom-call | tf_op jit(solution)/shard_map/processor/pallas_call | solution.py:349
  53.4 1.7 %copy.21 = bf16[256,512]{1,0:T(8,128)(2,1)} copy(bf16[256,512]{1,0:T(8,128)(2,1)} %get-tuple-element.8) | data formatting | bytes 524288
  55.1 2.3 %copy.22 = bf16[32,32,512]{2,1,0:T(8,128)(2,1)} copy(bf16[32,32,512]{2,1,0:T(8,128)(2,1)} %bitcast.13) | data formatting | bytes 2097152

commit v3 on v2

--- a/solution.py
+++ b/solution.py
@@ -10,7 +10,8 @@
 EPS = 1e-05
 BF = jnp.bfloat16
 F32 = jnp.float32
-ROWS = 256
+ROWS = 512
+EDGE_ROWS = 512
 LANES = 128
 
 
@@ -162,8 +163,8 @@
     l_ds = load(ds_h, ds)
     l_gs = load(gs_h, gs)
 
-    def rows_of(step):
-        return pl.ds(pl.multiple_of(step * ROWS, ROWS), ROWS)
+    def rows_of(step, size=ROWS):
+        return pl.ds(pl.multiple_of(step * size, size), size)
 
     columns_a = jnp.transpose(index_a[...]).astype(F32)
     shifted = [(columns_a - 256.0 * j).astype(BF) for j in range(-(-table_rows // 256))]
@@ -186,9 +187,9 @@
         table[0:own, :] = (0.5 * dot(nodes[...], ef[l, width : 2 * width, :])).astype(BF)
         table[table_rows:, :] = (0.5 * dot(nodes[...], ef[l, 2 * width :, :])).astype(BF)
 
-        @pl.loop(0, slots // ROWS)
+        @pl.loop(0, slots // EDGE_ROWS)
         def _(step):
-            rows = rows_of(step)
+            rows = rows_of(step, EDGE_ROWS)
             early[rows, :] = 0.5 * dot(edges[rows, :], ef[l, 0:width, :])
 
         l_nf[l].wait()
@@ -222,9 +223,9 @@
         table[own:table_rows, :] = (0.5 * dot(far, ef[l, width : 2 * width, :])).astype(BF)
         total[...] = jnp.zeros_like(total)
 
-        @pl.loop(0, slots // ROWS)
+        @pl.loop(0, slots // EDGE_ROWS)
         def _(step):
-            rows = rows_of(step)
+            rows = rows_of(step, EDGE_ROWS)
             hidden = silu(early[rows, :] + dot(pick[rows, :], table[...]))
             result = normalize(dot(hidden, es[l]))
             total[...] += dot(pick_t[:, rows], result.astype(BF))

time: 57.7 us -> 50.6 us (0.88)
  Pallas kernels: 52.8 us -> 45.7 us
    pallas_call x1, Pallas kernels: 52.8 us -> 45.7 us  [shards(): pl.pallas_call(functools.partial(kernel, dims), out_shape=(jax.ShapeDtype...]
where the time goes in v3:
time: 50.6 us; the launch traced here: 50.3 us
  Pallas kernels  45.7 us (90%)
  local copies, waits for them, and re-layouts  3.97 us (8%)
  between operations  0.65 us (1%)
    pallas_call x1, Pallas kernels, shards(): pl.pallas_call(functools.partial(kernel, dims), out_shape=(jax.ShapeDtype...  45.7 us
    unnamed x2, local copies, waits for them, and re-layouts  3.97 us

profile of v3, /device:TPU:0, one launch (start us, length us, event | category | flops | bytes accessed | tf_op | source)
XLA Modules:
  0.0 50.3 jit_solution(7206573934990171867)
XLA Ops:
  0.6 45.7 %processor.1 = (bf16[256,512]{1,0:T(8,128)(2,1)}, bf16[1024,512]{1,0:T(8,128)(2,1)}) custom-call(bf16[256,512]{1,0:T(8,128)(2,1)} %nodes_h.1, bf16[2048,512]{1,0:T(8,128)(2,1)} %edges_h.1, bf16[1024,512]{1,0:T(8,128)(2,1)} %bitcast.12, bf16[3072,512]{1,0:T(8,128)(2,1)} %bitcast.11, s32[16,128]{1,0:T(8,128)} %bitcast.14, s32[16,128]{1,0:T(8,128)} %bitcast.15, ...), custom_call_target="tpu_custom_call" | custom-call | tf_op jit(solution)/shard_map/processor/pallas_call | solution.py:350
  46.3 1.7 %copy.21 = bf16[256,512]{1,0:T(8,128)(2,1)} copy(bf16[256,512]{1,0:T(8,128)(2,1)} %get-tuple-element.8) | data formatting | bytes 524288
  48.0 2.3 %copy.22 = bf16[32,32,512]{2,1,0:T(8,128)(2,1)} copy(bf16[32,32,512]{2,1,0:T(8,128)(2,1)} %bitcast.13) | data formatting | bytes 2097152
